TPU v7x, 256 devices: a whole 4x4x8 slice. The times are simulated.
256 devices in a mesh: dp: 4 (over z_hi), row: 16 (over y, x), col: 4 (over z_lo, core).
Axes of the slice: x: 4, y: 4, z: 8 (z_hi: 4, z_lo: 2; z = z_hi * 2 + z_lo), core: 2. Of those that a mesh axis runs over, the one named last changes fastest.
Arguments:
- grad_partials: float32 [4, 4, 2048, 16384], P('dp', None, 'row', 'col'), may hold values from -300 to 300, as said below
- master_weights: float32 [8192, 16384], P(('dp', 'row'), 'col'), may hold values from -1.5 to 1.5
- row_moment: float32 [8192], P(('dp', 'row')), may hold values from 0.3 to 30
- col_moment: float32 [16384], P('col'), may hold values from 0.003 to 0.3
Outputs:
- new_master: float32 [8192, 16384], P(('dp', 'row'), 'col')
- new_row_moment: float32 [8192], P(('dp', 'row'))
- new_col_moment: float32 [16384], P('col')
- compute_weights: bfloat16 [4, 2048, 16384], P(None, 'row', 'col')
- rms_update: float32 [], replicated
Inputs may be any that keep to these rules, and one draw needn't show every extreme that they name: `grad_partials`: finite gradient partials.
All inputs are finite; a program needn't handle non-finite values.
Results may differ from a plain program's by a relative error of at most 0.0004.
Values may be sent and summed in bfloat16 or wider, within the bound.
A program may use at most 128 MiB of HBM per device.

v0:
```python
import jax
import jax.numpy as jnp
from jax import lax
from jax.sharding import PartitionSpec as P

decay_rate = 0.9
step_rate = 0.05
tiny_value = 1e-30


def local(grad_partials, master_weights, row_moment, col_moment):
    local_grads = grad_partials[0]
    row_dev = master_weights.shape[0]
    col_dev = master_weights.shape[1]
    groups = lax.axis_size("dp")
    all_rows = row_dev * groups * lax.axis_size("row")
    full_width = col_dev * lax.axis_size("col")
    summed = lax.psum_scatter(local_grads, "dp", scatter_dimension=0, tiled=True)
    gradient = summed.reshape(row_dev, col_dev)
    weights_all, moments_all = (master_weights, row_moment)
    squared = gradient * gradient
    row_totals = lax.psum(jnp.sum(squared, axis=1), "col")
    local_cols = jnp.sum(squared, axis=0)
    row_mean = row_totals / full_width + tiny_value
    new_rows = decay_rate * moments_all + (1.0 - decay_rate) * row_mean
    rows_sum = jnp.sum(new_rows)
    col_totals, moment_sum = lax.psum((local_cols, rows_sum), ("dp", "row"))
    col_mean = col_totals / all_rows + tiny_value
    new_cols = decay_rate * col_moment + (1.0 - decay_rate) * col_mean
    scale_mean = moment_sum / all_rows
    update = gradient * lax.rsqrt(new_rows[:, None] * new_cols[None, :] / scale_mean)
    update_local = jnp.sum(update * update)
    update_sum = lax.psum(update_local, ("dp", "row", "col"))
    entry_count = float(all_rows * full_width)
    rms_update = jnp.sqrt(update_sum / entry_count)
    new_weights = weights_all - step_rate * update / jnp.maximum(1.0, rms_update)
    copies = lax.all_gather(new_weights.astype(jnp.bfloat16)[None], "dp", axis=0, tiled=True)
    return (new_weights, new_rows, new_cols, copies, rms_update)


def solution(mesh):
    return jax.shard_map(
        local,
        mesh=mesh,
        in_specs=(P("dp", None, "row", "col"), P(("dp", "row"), "col"), P(("dp", "row")), P("col")),
        out_specs=(P(("dp", "row"), "col"), P(("dp", "row")), P("col"), P(None, "row", "col"), P()),
        check_vma=False,
    )
```

profile of v0, /device:TPU:37, one launch (start us, length us, event | category | flops | bytes accessed | tf_op | source)
XLA Modules:
  0.0 726.3 jit_solution(2824089146126804063)
XLA Ops:
  7.2 0.0 reduce-scatter.2.cloned.1.call-start
  7.2 0.7 reduce-scatter.2.cloned.1.call-update
  7.9 0.0 copy-start.4
  7.9 0.0 copy-start.2
  7.9 0.0 all-gather.3.cloned.1.call-start
  8.0 155.5 %reduce-scatter.2.cloned.1.call-done = f32[1,128,4096]{2,1,0:T(8,128)} async-done(((f32[4,128,4096]{2,1,0:T(8,128)}), f32[1,128,4096]{2,1,0:T(8,128)}) %reduce-scatter.2.cloned.1.call-update) | async-done | bytes 2097168 | tf_op jit(solution)/shard_map/reduce_scatter | solution.py:18
  163.5 0.0 copy-start
  163.5 2.0 fusion
  165.5 9.4 %psum.28 = f32[128]{0:T(128)S(1)} all-reduce(f32[128]{0:T(128)S(1)} %get-tuple-element.6), channel_id=1, replica_groups=mesh['dp'=4,'row'=16,'col'=4] {'col'}, use_global_device_ids=true, to_apply=%region_2.0 | all-reduce | flops 128 | bytes 1024 | tf_op jit(solution)/shard_map/psum | solution.py:22
  174.9 0.0 copy-done.4
  174.9 0.6 fusion.3
  175.5 0.0 copy-start.3
  175.5 313.2 %all-reduce = (f32[]{:T(128)}, f32[4096]{0:T(1024)S(1)}) all-reduce(f32[]{:T(128)} %get-tuple-element.11, f32[4096]{0:T(1024)S(1)} %get-tuple-element.5), channel_id=1, replica_groups=mesh['dp'=4,'row'=16,'col'=4] {'dp','row'}, use_global_device_ids=true, to_apply=%region_6.0 | all-reduce | flops 4097 | bytes 32776 | tf_op jit(solution)/shard_map/psum | solution.py:27
  489.4 0.0 copy-done.2
  489.4 0.0 copy-start.1
  489.4 0.0 copy-done
  489.4 1.2 multiply_reduce_fusion
  490.6 134.0 %psum.31 = f32[]{:T(128)} all-reduce(f32[]{:T(128)} %multiply_reduce_fusion), channel_id=1, replica_groups=mesh['dp'=4,'row'=16,'col'=4] {'dp','row','col'}, use_global_device_ids=true, to_apply=%region_8.0 | all-reduce | flops 1 | bytes 8 | tf_op jit(solution)/shard_map/psum | solution.py:33
  625.4 3.9 fusion.2
  629.3 0.0 copy-done.3
  629.3 0.0 copy-done.1
  629.3 0.0 all-gather.3.cloned.1.call-update
  629.3 84.4 %all-gather.3.cloned.1.call-done = bf16[512,4096]{1,0:T(8,128)(2,1)} async-done(((bf16[128,4096]{1,0:T(8,128)(2,1)}), bf16[512,4096]{1,0:T(8,128)(2,1)}) %all-gather.3.cloned.1.call-update) | async-done | bytes 4194320 | tf_op jit(solution)/shard_map/all_gather | solution.py:37
  713.6 4.7 copy.10
  (1 shorter events, 0.0 us)
Async XLA Ops:
  7.2 156.3 %reduce-scatter.2.cloned.1.call-start = ((), (), s32[]{:S(2)}) async-start(), calls=%async_computation.1 | async-start | bytes 10485760 | tf_op jit(solution)/shard_map/reduce_scatter | solution.py:18
  7.9 167.0 %copy-start.4 = (f32[128]{0:T(128)S(1)}, f32[128]{0:T(128)}, u32[]{:S(2)}) copy-start(f32[128]{0:T(128)} %param.6) | copy-start | bytes 1540
  7.9 481.4 %copy-start.2 = (f32[4096]{0:T(1024)S(1)}, f32[4096]{0:T(1024)}, u32[]{:S(2)}) copy-start(f32[4096]{0:T(1024)} %param.7) | copy-start | bytes 49156
  7.9 705.7 %all-gather.3.cloned.1.call-start = ((), (), s32[]{:S(2)}) async-start(), calls=%async_computation.2 | async-start | bytes 5242880 | tf_op jit(solution)/shard_map/all_gather | solution.py:37
  163.5 325.9 %copy-start = (f32[1,128,4096]{2,1,0:T(8,128)S(1)}, f32[1,128,4096]{2,1,0:T(8,128)}, u32[]{:S(2)}) copy-start(f32[1,128,4096]{2,1,0:T(8,128)} %reduce-scatter.2.cloned.1.call-done) | copy-start | bytes 6291460
  175.5 453.8 %copy-start.3 = (f32[128]{0:T(128)}, f32[128]{0:T(128)S(1)}, u32[]{:S(2)}) copy-start(f32[128]{0:T(128)S(1)} %get-tuple-element.19) | copy-start | bytes 1540
  489.4 139.9 %copy-start.1 = (f32[4096]{0:T(1024)}, f32[4096]{0:T(1024)S(1)}, u32[]{:S(2)}) copy-start(f32[4096]{0:T(1024)S(1)} %multiply_add_fusion) | copy-start | bytes 49156
Sparse Core Ops, SparseCore 0:
  10.6 152.8 reduce-scatter.1
  629.4 84.1 all-gather.2
where the time goes:
time: 727 us; the launch traced here: 726 us
  blocking collectives  457 us (63%)
  waiting for transfers between devices  241 us (33%)
  between operations  16.6 us (2%)
  other arithmetic  7.76 us (1%)
    psum x1, blocking collectives, local(): col_totals, moment_sum = lax.psum((local_cols, rows_sum), ('dp', 'row'))  313 us
    reduce_scatter x1, waiting for transfers between devices, local(): lax.psum_scatter(local_grads, 'dp', scatter_dimension=0, tiled=True)  155 us
    psum x1, blocking collectives, local(): update_sum = lax.psum(update_local, ('dp', 'row', 'col'))  134 us
    all_gather x1, waiting for transfers between devices, local(): lax.all_gather(new_weights.astype(jnp.bfloat16)[None], 'dp', axis=0, tile...  84.4 us
  transfers between devices with their start and end apart: 2, of which 2 were waited for; matrix products, arithmetic and copies ran while one was open for 0% of the time, Pallas kernels for 0%

commit v1 on v0

--- a/solution.py
+++ b/solution.py
@@ -24,7 +24,9 @@
     row_mean = row_totals / full_width + tiny_value
     new_rows = decay_rate * moments_all + (1.0 - decay_rate) * row_mean
     rows_sum = jnp.sum(new_rows)
-    col_totals, moment_sum = lax.psum((local_cols, rows_sum), ("dp", "row"))
+    col_totals, moment_sum = lax.psum(
+        lax.psum((local_cols, rows_sum), axis_name="row"), axis_name="dp"
+    )
     col_mean = col_totals / all_rows + tiny_value
     new_cols = decay_rate * col_moment + (1.0 - decay_rate) * col_mean
     scale_mean = moment_sum / all_rows

time: 727 us -> 445 us (0.61)
  blocking collectives: 457 us -> 173 us
    psum x1 -> x2, blocking collectives: 313 us -> 70.7 us  [the longest x1 56.2 us: local(): lax.psum((local_cols, rows_sum), axis_name='row')]
    psum x1, blocking collectives: 134 us -> 93.4 us  [local(): update_sum = lax.psum(update_local, ('dp', 'row', 'col'))]
where the time goes in v1:
time: 445 us; the launch traced here: 444 us
  waiting for transfers between devices  242 us (54%)
  blocking collectives  173 us (39%)
  between operations  16.6 us (4%)
  other arithmetic  7.76 us (2%)
  local copies, waits for them, and re-layouts  4.72 us (1%)
    reduce_scatter x1, waiting for transfers between devices, local(): lax.psum_scatter(local_grads, 'dp', scatter_dimension=0, tiled=True)  155 us
    psum x1, blocking collectives, local(): update_sum = lax.psum(update_local, ('dp', 'row', 'col'))  93.4 us
    all_gather x1, waiting for transfers between devices, local(): lax.all_gather(new_weights.astype(jnp.bfloat16)[None], 'dp', axis=0, tile...  85.6 us
    psum x1, blocking collectives, local(): lax.psum((local_cols, rows_sum), axis_name='row')  56.2 us
    psum x1, blocking collectives, local(): lax.psum(lax.psum((local_cols, rows_sum), axis_name='row'), axis_name='dp')  14.5 us
    psum x1, blocking collectives, local(): row_totals = lax.psum(jnp.sum(squared, axis=1), 'col')  9.37 us
  transfers between devices with their start and end apart: 2, of which 2 were waited for; matrix products, arithmetic and copies ran while one was open for 0% of the time, Pallas kernels for 0%

profile of v1, /device:TPU:37, one launch (start us, length us, event | category | flops | bytes accessed | tf_op | source)
XLA Modules:
  0.0 444.4 jit_solution(15271801691491041260)
XLA Ops:
  7.2 0.0 reduce-scatter.2.cloned.1.call-start
  7.2 0.7 reduce-scatter.2.cloned.1.call-update
  7.9 0.0 copy-start.4
  7.9 0.0 copy-start.2
  7.9 0.0 all-gather.3.cloned.1.call-start
  8.0 155.5 %reduce-scatter.2.cloned.1.call-done = f32[1,128,4096]{2,1,0:T(8,128)} async-done(((f32[4,128,4096]{2,1,0:T(8,128)}), f32[1,128,4096]{2,1,0:T(8,128)}) %reduce-scatter.2.cloned.1.call-update) | async-done | bytes 2097168 | tf_op jit(solution)/shard_map/reduce_scatter | solution.py:18
  163.5 0.0 copy-start
  163.5 2.0 fusion
  165.5 9.4 %psum.42 = f32[128]{0:T(128)S(1)} all-reduce(f32[128]{0:T(128)S(1)} %get-tuple-element.6), channel_id=1, replica_groups=mesh['dp'=4,'row'=16,'col'=4] {'col'}, use_global_device_ids=true, to_apply=%region_2.0 | all-reduce | flops 128 | bytes 1024 | tf_op jit(solution)/shard_map/psum | solution.py:22
  174.9 0.0 copy-done.4
  174.9 0.6 fusion.3
  175.5 0.0 copy-start.3
  175.5 56.2 %all-reduce = (f32[]{:T(128)}, f32[4096]{0:T(1024)S(1)}) all-reduce(f32[]{:T(128)} %get-tuple-element.13, f32[4096]{0:T(1024)S(1)} %get-tuple-element.5), channel_id=1, replica_groups=mesh['dp'=4,'row'=16,'col'=4] {'row'}, use_global_device_ids=true, to_apply=%region_7.0 | all-reduce | flops 4097 | bytes 32776 | tf_op jit(solution)/shard_map/psum | solution.py:28
  231.7 14.5 %all-reduce.1 = (f32[]{:T(128)}, f32[4096]{0:T(1024)S(1)}) all-reduce(f32[]{:T(128)} %get-tuple-element.7, f32[4096]{0:T(1024)S(1)} %get-tuple-element.8), channel_id=1, replica_groups=mesh['dp'=4,'row'=16,'col'=4] {'dp'}, use_global_device_ids=true, to_apply=%region_8.0 | all-reduce | flops 4097 | bytes 32776 | tf_op jit(solution)/shard_map/psum | solution.py:27
  246.9 0.0 copy-done.2
  246.9 0.0 copy-start.1
  246.9 0.0 copy-done
  246.9 1.2 multiply_reduce_fusion
  248.2 93.4 %psum.47 = f32[]{:T(128)} all-reduce(f32[]{:T(128)} %multiply_reduce_fusion), channel_id=1, replica_groups=mesh['dp'=4,'row'=16,'col'=4] {'dp','row','col'}, use_global_device_ids=true, to_apply=%region_10.0 | all-reduce | flops 1 | bytes 8 | tf_op jit(solution)/shard_map/psum | solution.py:35
  342.2 3.9 fusion.2
  346.1 0.0 copy-done.3
  346.1 0.0 copy-done.1
  346.1 0.0 all-gather.3.cloned.1.call-update
  346.1 85.6 %all-gather.3.cloned.1.call-done = bf16[512,4096]{1,0:T(8,128)(2,1)} async-done(((bf16[128,4096]{1,0:T(8,128)(2,1)}), bf16[512,4096]{1,0:T(8,128)(2,1)}) %all-gather.3.cloned.1.call-update) | async-done | bytes 4194320 | tf_op jit(solution)/shard_map/all_gather | solution.py:39
  431.7 4.7 %copy.10 = bf16[4,128,4096]{2,1,0:T(8,128)(2,1)} copy(bf16[4,128,4096]{2,1,0:T(8,128)(2,1)} %bitcast.15) | data formatting | bytes 8388608
  (1 shorter events, 0.0 us)
Async XLA Ops:
  7.2 156.3 %reduce-scatter.2.cloned.1.call-start = ((), (), s32[]{:S(2)}) async-start(), calls=%async_computation.1 | async-start | bytes 10485760 | tf_op jit(solution)/shard_map/reduce_scatter | solution.py:18
  7.9 167.0 %copy-start.4 = (f32[128]{0:T(128)S(1)}, f32[128]{0:T(128)}, u32[]{:S(2)}) copy-start(f32[128]{0:T(128)} %param.6) | copy-start | bytes 1540
  7.9 239.0 %copy-start.2 = (f32[4096]{0:T(1024)S(1)}, f32[4096]{0:T(1024)}, u32[]{:S(2)}) copy-start(f32[4096]{0:T(1024)} %param.7) | copy-start | bytes 49156
  7.9 423.8 %all-gather.3.cloned.1.call-start = ((), (), s32[]{:S(2)}) async-start(), calls=%async_computation.2 | async-start | bytes 5242880 | tf_op jit(solution)/shard_map/all_gather | solution.py:39
  163.5 83.5 %copy-start = (f32[1,128,4096]{2,1,0:T(8,128)S(1)}, f32[1,128,4096]{2,1,0:T(8,128)}, u32[]{:S(2)}) copy-start(f32[1,128,4096]{2,1,0:T(8,128)} %reduce-scatter.2.cloned.1.call-done) | copy-start | bytes 6291460
  175.5 170.6 %copy-start.3 = (f32[128]{0:T(128)}, f32[128]{0:T(128)S(1)}, u32[]{:S(2)}) copy-start(f32[128]{0:T(128)S(1)} %get-tuple-element.21) | copy-start | bytes 1540
  246.9 99.2 %copy-start.1 = (f32[4096]{0:T(1024)}, f32[4096]{0:T(1024)S(1)}, u32[]{:S(2)}) copy-start(f32[4096]{0:T(1024)S(1)} %multiply_add_fusion) | copy-start | bytes 49156
Sparse Core Ops, SparseCore 0:
  10.6 152.8 reduce-scatter.1
  346.2 85.4 all-gather.2
